TPU v7x, 32 devices: a whole 2x2x4 slice. The times are simulated.
32 devices in a mesh: fsdp: 2 (over x), rep: 16 (over z, y, core).
Axes of the slice: x: 2, y: 2, z: 4, core: 2. Of those that a mesh axis runs over, the one named last changes fastest.
Arguments:
- images: bfloat16 [128, 197, 384], P(('fsdp', 'rep')), may hold values from -5 to 5
- cotangent: bfloat16 [128, 197, 384], P(('fsdp', 'rep')), may hold values from -6 to 6
- weights: float32 [1777664], P('fsdp'), may hold values from -3 to 3
- first_moment: float32 [1777664], P(('fsdp', 'rep'))
- second_moment: float32 [1777664], P(('fsdp', 'rep')), as said below
Outputs:
- output: bfloat16 [128, 197, 384], P(('fsdp', 'rep'))
- input_grad: bfloat16 [128, 197, 384], P(('fsdp', 'rep'))
- new_weights: float32 [1777664], P('fsdp')
- gradients: float32 [1777664], P(('fsdp', 'rep'))
- new_first: float32 [1777664], P(('fsdp', 'rep'))
- new_second: float32 [1777664], P(('fsdp', 'rep'))
Inputs may be any that keep to these rules, and one draw needn't show every extreme that they name: second_moment is positive.
All inputs are finite; a program needn't handle non-finite values.
Results may differ from a plain program's by a relative error of at most 0.0095.
The roundings to bfloat16 on the way count: a program that leaves them out, or rounds other values in their place, can miss the bound.
Values may be sent and summed in bfloat16 or wider, within the bound.
A program may use at most 128 MiB of HBM per device.

v0:
```python
import functools

import jax
import jax.numpy as jnp
from jax import lax
from jax.experimental import pallas as pl
from jax.experimental.pallas import tpu as pltpu
from jax.sharding import PartitionSpec as P

D = 384
H = 6
FF = 1536
LANES = 128

norm_eps = 1e-06
half_root = 0.7071067811865476
inv_root_two_pi = 0.3989422804014327
beta_one = 0.9
beta_two = 0.999
learn_rate = 0.02
decay_rate = 0.05
adam_eps = 1e-08

AT_QKV = 0
AT_PROJ = AT_QKV + 3 * D * D // LANES
AT_FC1 = AT_PROJ + D * D // LANES
AT_FC2 = AT_FC1 + D * FF // LANES
AT_VEC = AT_FC2 + FF * D // LANES
AT_B1 = AT_VEC + 8 * D // LANES
AT_TAIL = AT_B1 + FF // LANES

BF = jnp.bfloat16
F32 = jnp.float32


def nn(a, b):
    return lax.dot_general(a, b, (((1,), (0,)), ((), ())), preferred_element_type=F32)


def nt(a, b):
    return lax.dot_general(a, b, (((1,), (1,)), ((), ())), preferred_element_type=F32)


def tn(a, b):
    return lax.dot_general(a, b, (((0,), (0,)), ((), ())), preferred_element_type=F32)


def normalize(values):
    centred = values - jnp.mean(values, -1, keepdims=True)
    inverse = lax.rsqrt(jnp.mean(centred * centred, -1, keepdims=True) + norm_eps)
    return centred * inverse, inverse


def normalize_back(d_scaled, scaled, inverse):
    first_mean = jnp.mean(d_scaled, -1, keepdims=True)
    second_mean = jnp.mean(d_scaled * scaled, -1, keepdims=True)
    return (d_scaled - first_mean - scaled * second_mean) * inverse


def columns(x):
    return jnp.sum(x, 0, keepdims=True)


def unpack_into(flat, wq, wp, w1, w2, vec, b1):
    for ref, base in ((wq, AT_QKV), (wp, AT_PROJ), (w1, AT_FC1), (w2, AT_FC2)):
        rows, blocks = ref.shape[0], ref.shape[1] // LANES
        for j in range(blocks):
            ref[:, j * LANES : (j + 1) * LANES] = flat[pl.ds(base + j, rows, stride=blocks), :].astype(BF)
    for c in range(D // LANES):
        vec[:, c * LANES : (c + 1) * LANES] = flat[pl.ds(AT_VEC + c, 8, stride=D // LANES), :]
    for c in range(FF // LANES):
        b1[:, c * LANES : (c + 1) * LANES] = flat[AT_B1 + c : AT_B1 + c + 1, :]


def pack_into(flat, aq, ap, a1, a2, avec, ab1):
    for ref, base in ((aq, AT_QKV), (ap, AT_PROJ), (a1, AT_FC1), (a2, AT_FC2)):
        rows, blocks = ref.shape[0], ref.shape[1] // LANES
        for j in range(blocks):
            flat[pl.ds(base + j, rows, stride=blocks), :] = ref[:, j * LANES : (j + 1) * LANES]
    for c in range(D // LANES):
        flat[pl.ds(AT_VEC + c, 8, stride=D // LANES), :] = avec[:, c * LANES : (c + 1) * LANES]
    for c in range(FF // LANES):
        flat[AT_B1 + c : AT_B1 + c + 1, :] = ab1[:, c * LANES : (c + 1) * LANES]
    flat[AT_TAIL:, :] = jnp.zeros((flat.shape[0] - AT_TAIL, LANES), F32)


def image_step(seq, img, cot, out, dinp, wq, wp, w1, w2, vec, b1, aq, ap, a1, a2, avec, ab1, xs, gs, pf):
    pad = xs.shape[0]
    xs[0:seq, :] = img[0].astype(F32)
    gs[0:seq, :] = cot[0].astype(F32)
    x = xs[...]
    xhat1, inv1 = normalize(x)
    normed1 = (xhat1 * vec[0:1, :] + vec[1:2, :]).astype(BF)
    q = (nn(normed1, wq[:, :D]) + vec[2:3, :]).astype(BF)
    k = nn(normed1, wq[:, D : 2 * D]).astype(BF)
    v = (nn(normed1, wq[:, 2 * D :]) + vec[3:4, :]).astype(BF)
    scale = (D // H) ** (-0.5)
    lane = lax.broadcasted_iota(jnp.int32, (1, LANES), 1)
    halves = [(lane < 64), (lane >= 64)]
    key_ok = lax.broadcasted_iota(jnp.int32, (1, pad), 1) < seq

    def half(block, i):
        return jnp.where(halves[i], block, jnp.zeros_like(block))

    mixed_blocks = []
    for pair in range(D // LANES):
        cut = slice(pair * LANES, (pair + 1) * LANES)
        total = None
        for i in range(2):
            s = nt(half(q[:, cut], i), k[:, cut]) * scale
            s = jnp.where(key_ok, s, -1e30)
            e = jnp.exp(s - jnp.max(s, -1, keepdims=True))
            p = e * (1.0 / jnp.sum(e, -1, keepdims=True))
            pf[2 * pair + i] = p
            term = nn(p.astype(BF), half(v[:, cut], i))
            total = term if total is None else total + term
        mixed_blocks.append(total.astype(BF))
    mixed = jnp.concatenate(mixed_blocks, 1)
    resid = x + nn(mixed, wp[...]) + vec[4:5, :]
    xhat2, inv2 = normalize(resid)
    normed2 = (xhat2 * vec[5:6, :] + vec[6:7, :]).astype(BF)
    dout_f = gs[...]
    dout = dout_f.astype(BF)
    result = resid + vec[7:8, :]
    dnorm2 = None
    step = 512
    for c in range(0, FF, step):
        cut = slice(c, c + step)
        pre = nn(normed2, w1[:, cut]) + b1[:, cut]
        cdf = 0.5 * (1.0 + lax.erf(pre * half_root))
        act = (pre * cdf).astype(BF)
        result = result + nn(act, w2[cut, :])
        a2[cut, :] += tn(act, dout)
        dact = nt(dout, w2[cut, :])
        dpre = dact * (cdf + pre * jnp.exp(-0.5 * pre * pre) * inv_root_two_pi)
        ab1[:, cut] += columns(dpre)
        dpre_b = dpre.astype(BF)
        a1[:, cut] += tn(normed2, dpre_b)
        term = nt(dpre_b, w1[:, cut])
        dnorm2 = term if dnorm2 is None else dnorm2 + term
    out[0] = result.astype(BF)[0:seq, :]
    avec[7:8, :] += columns(dout_f)
    avec[5:6, :] += columns(dnorm2 * xhat2)
    avec[6:7, :] += columns(dnorm2)
    dresid = dout_f + normalize_back(dnorm2 * vec[5:6, :], xhat2, inv2)
    avec[4:5, :] += columns(dresid)
    dresid_b = dresid.astype(BF)
    ap[...] += tn(mixed, dresid_b)
    dmixed = nt(dresid_b, wp[...]).astype(BF)
    dq_blocks, dk_blocks, dv_blocks = [], [], []
    for pair in range(D // LANES):
        cut = slice(pair * LANES, (pair + 1) * LANES)
        dq = dk = dv = None
        for i in range(2):
            p = pf[2 * pair + i]
            dm = half(dmixed[:, cut], i)
            dp = nt(dm, v[:, cut])
            delta = jnp.sum(p * dp, -1, keepdims=True)
            ds = (p * (dp - delta) * scale).astype(BF)
            terms = (
                nn(ds, half(k[:, cut], i)),
                tn(ds, half(q[:, cut], i)),
                tn(p.astype(BF), dm),
            )
            if dq is None:
                dq, dk, dv = terms
            else:
                dq, dk, dv = dq + terms[0], dk + terms[1], dv + terms[2]
        avec[2:3, cut] += columns(dq)
        avec[3:4, cut] += columns(dv)
        dq_blocks.append(dq.astype(BF))
        dk_blocks.append(dk.astype(BF))
        dv_blocks.append(dv.astype(BF))
    dnorm1 = None
    for part, blocks in enumerate((dq_blocks, dk_blocks, dv_blocks)):
        cut = slice(part * D, (part + 1) * D)
        d_part = jnp.concatenate(blocks, 1)
        aq[:, cut] += tn(normed1, d_part)
        term = nt(d_part, wq[:, cut])
        dnorm1 = term if dnorm1 is None else dnorm1 + term
    avec[0:1, :] += columns(dnorm1 * xhat1)
    avec[1:2, :] += columns(dnorm1)
    dx = dresid + normalize_back(dnorm1 * vec[0:1, :], xhat1, inv1)
    dinp[0] = dx.astype(BF)[0:seq, :]


def compute_kernel(seq, img, cot, pflat, out, dinp, gflat, wq, wp, w1, w2, vec, b1, aq, ap, a1, a2, avec, ab1, xs, gs, pf):
    @pl.when(pl.program_id(0) == 0)
    def _():
        gflat[...] = pflat[...].astype(F32)
        unpack_into(gflat, wq, wp, w1, w2, vec, b1)
        for ref in (aq, ap, a1, a2, avec, ab1, xs, gs):
            ref[...] = jnp.zeros_like(ref)

    image_step(seq, img, cot, out, dinp, wq, wp, w1, w2, vec, b1, aq, ap, a1, a2, avec, ab1, xs, gs, pf)

    @pl.when(pl.program_id(0) == pl.num_programs(0) - 1)
    def _():
        pack_into(gflat, aq, ap, a1, a2, avec, ab1)


def compute(images, cotangent, params):
    batch, seq, width = images.shape
    pad = (seq + 15) // 16 * 16
    rows = params.shape[0]
    per_image = pl.BlockSpec((1, seq, width), lambda i: (i, 0, 0))
    whole = pl.BlockSpec(memory_space=pltpu.VMEM)
    mats = [(D, 3 * D), (D, D), (D, FF), (FF, D)]
    vecs = [(8, D), (1, FF)]
    return pl.pallas_call(
        functools.partial(compute_kernel, seq),
        grid=(batch,),
        in_specs=[per_image, per_image, whole],
        out_specs=[per_image, per_image, whole],
        out_shape=[
            jax.ShapeDtypeStruct(images.shape, BF),
            jax.ShapeDtypeStruct(images.shape, BF),
            jax.ShapeDtypeStruct((rows, LANES), F32),
        ],
        scratch_shapes=[pltpu.VMEM(s, BF) for s in mats]
        + [pltpu.VMEM(s, F32) for s in vecs]
        + [pltpu.VMEM(s, F32) for s in mats + vecs]
        + [pltpu.VMEM((pad, width), F32)] * 2
        + [pltpu.VMEM((H, pad, pad), F32)],
        compiler_params=pltpu.CompilerParams(vmem_limit_bytes=60 * 2**20),
    )(images, cotangent, params)


def adamw(weight_vals, grad_vals, first_vals, second_vals):
    first_new = beta_one * first_vals + (1.0 - beta_one) * grad_vals
    second_new = beta_two * second_vals + (1.0 - beta_two) * grad_vals * grad_vals
    first_hat = first_new / (1.0 - beta_one**2)
    second_hat = second_new / (1.0 - beta_two**2)
    change = -learn_rate * (first_hat / (jnp.sqrt(second_hat) + adam_eps) + decay_rate * weight_vals)
    return (change, first_new, second_new)


def on_device(images, cotangent, weights, first_moment, second_moment):
    half_bf = weights.astype(BF)
    params = lax.all_gather(half_bf, "fsdp", axis=0, tiled=True).reshape(-1, LANES)
    output, input_grad, flat_grad = compute(images, cotangent, params)
    own_grad = lax.psum_scatter(
        flat_grad.reshape(-1).astype(BF), ("fsdp", "rep"), scatter_dimension=0, tiled=True
    ).astype(F32)
    piece_len = first_moment.shape[0]
    offset = lax.axis_index("rep") * piece_len
    own_weights = lax.dynamic_slice_in_dim(weights, offset, piece_len)
    change, new_first, new_second = adamw(own_weights, own_grad, first_moment, second_moment)
    changes = lax.all_gather(change.astype(BF), "rep", axis=0, tiled=True)
    new_weights = weights + changes.astype(F32)
    return (output, input_grad, new_weights, own_grad, new_first, new_second)


def solution(mesh):
    in_specs = (
        P(("fsdp", "rep"), None, None),
        P(("fsdp", "rep"), None, None),
        P("fsdp"),
        P(("fsdp", "rep")),
        P(("fsdp", "rep")),
    )
    out_specs = (
        P(("fsdp", "rep"), None, None),
        P(("fsdp", "rep"), None, None),
        P("fsdp"),
        P(("fsdp", "rep")),
        P(("fsdp", "rep")),
        P(("fsdp", "rep")),
    )
    return jax.shard_map(
        on_device, mesh=mesh, in_specs=in_specs, out_specs=out_specs, check_vma=False
    )
```

profile of v0, /device:TPU:1, one launch (start us, length us, event | category | flops | bytes accessed | tf_op | source)
XLA Modules:
  0.0 310.1 jit_solution(6978834919945159839)
XLA Ops:
  7.2 0.0 copy-start.1
  7.2 0.0 copy-start.2
  7.2 0.0 all-gather.4.cloned.1.call-start
  7.2 3.5 %convert_element_type.18 = bf16[888832]{0:T(1024)(128)(2,1)} convert(f32[888832]{0:T(1024)} %param.7) | non-fusion elementwise | flops 888832 | bytes 5332992 | tf_op jit(solution)/shard_map/convert_element_type | solution.py:239
  10.7 0.0 all-gather.4.cloned.1.call-update
  10.7 0.0 all-reduce.3.cloned.1.call-start
  10.8 0.0 copy-done.1
  10.8 0.9 copy.15.img
  11.7 0.0 copy-done.2
  11.7 0.9 copy.16.cot
  12.6 49.7 %all-gather.4.cloned.1.call-done = bf16[1777664]{0:T(1024)(128)(2,1)} async-done(((bf16[888832]{0:T(1024)(128)(2,1)}), bf16[1777664]{0:T(1024)(128)(2,1)}) %all-gather.4.cloned.1.call-update) | async-done | bytes 3555344 | tf_op jit(solution)/shard_map/all_gather | solution.py:240
  62.3 38.4 %shard_map.100 = (bf16[4,197,384]{2,1,0:T(8,128)(2,1)}, bf16[4,197,384]{2,1,0:T(8,128)(2,1)}, f32[13888,128]{1,0:T(8,128)}) custom-call(bf16[4,197,384]{2,1,0:T(8,128)(2,1)} %copy.15.img, bf16[4,197,384]{2,1,0:T(8,128)(2,1)} %copy.16.cot, bf16[13888,128]{1,0:T(8,128)(2,1)} %bitcast.5), custom_call_target="tpu_custom_call" | custom-call | tf_op jit(solution)/shard_map/pallas_call | solution.py:210
  100.7 4.5 %convert_bitcast_fusion = bf16[1777664]{0:T(1024)(128)(2,1)} fusion(f32[13888,128]{1,0:T(8,128)} %get-tuple-element.11), kind=kLoop, calls=%fused_computation | loop fusion | flops 1777664 | bytes 10665984 | tf_op jit(solution)/shard_map/convert_element_type | solution.py:243
  105.2 0.0 copy-start
  105.2 0.0 all-reduce.3.cloned.1.call-update
  105.2 0.2 all-gather.6.cloned.1.call-start
  105.4 138.6 %all-reduce.3.cloned.1.call-done = bf16[1777664]{0:T(1024)(128)(2,1)} async-done(((bf16[1777664]{0:T(1024)(128)(2,1)}), bf16[1777664]{0:T(1024)(128)(2,1)}) %all-reduce.3.cloned.1.call-update) | async-done | bytes 3555344
  244.1 0.0 copy-done
  244.1 2.2 multiply_convert_fusion
  246.2 0.8 reshape.18
  247.0 0.0 all-gather.6.cloned.1.call-update
  247.1 2.1 copy.17
  249.2 2.1 copy.18
  251.3 44.4 %all-gather.6.cloned.1.call-done = bf16[16,1,55552]{2,1,0:T(2,128)(2,1)} async-done(((bf16[1,1,55552]{2,1,0:T(2,128)(2,1)}), bf16[16,1,55552]{2,1,0:T(2,128)(2,1)}) %all-gather.6.cloned.1.call-update) | async-done | bytes 1777680 | tf_op jit(solution)/shard_map/all_gather | solution.py:249
  295.7 5.7 %convert_element_type.24 = f32[16,1,55552]{2,1,0:T(1,128)S(1)} convert(bf16[16,1,55552]{2,1,0:T(2,128)(2,1)} %all-gather.6.cloned.1.call-done) | non-fusion elementwise | flops 888832 | bytes 5332992 | tf_op jit(solution)/shard_map/convert_element_type | solution.py:250
  301.4 2.2 add.29
Async XLA Ops:
  7.2 3.6 %copy-start.1 = (bf16[4,197,384]{2,0,1:T(4,128)(2,1)S(1)}, bf16[4,197,384]{2,0,1:T(4,128)(2,1)}, u32[]{:S(2)}) copy-start(bf16[4,197,384]{2,0,1:T(4,128)(2,1)} %param.5) | copy-start | bytes 1815556
  7.2 4.5 %copy-start.2 = (bf16[4,197,384]{2,0,1:T(4,128)(2,1)S(1)}, bf16[4,197,384]{2,0,1:T(4,128)(2,1)}, u32[]{:S(2)}) copy-start(bf16[4,197,384]{2,0,1:T(4,128)(2,1)} %param.6) | copy-start | bytes 1815556
  7.2 55.1 %all-gather.4.cloned.1.call-start = ((), (), s32[]{:S(2)}) async-start(), calls=%async_computation | async-start | bytes 5332992 | tf_op jit(solution)/shard_map/all_gather | solution.py:240
  10.7 233.3 %all-reduce.3.cloned.1.call-start = ((), (), s32[]{:S(2)}) async-start(), calls=%async_computation.2 | async-start | bytes 7110656
  105.2 138.9 %copy-start = (f32[888832]{0:T(1024)S(1)}, f32[888832]{0:T(1024)}, u32[]{:S(2)}) copy-start(f32[888832]{0:T(1024)} %param.7) | copy-start | bytes 10665988
  105.2 190.5 %all-gather.6.cloned.1.call-start = ((), (), s32[]{:S(2)}) async-start(), calls=%async_computation.1 | async-start | bytes 3777536 | tf_op jit(solution)/shard_map/all_gather | solution.py:249
Sparse Core Ops, SparseCore 0:
  10.9 51.4 all-gather.3
  105.3 138.7 all-reduce.2
  247.2 48.5 all-gather.5
where the time goes:
time: 311 us; the launch traced here: 310 us
  waiting for transfers between devices  233 us (75%)
  Pallas kernels  38.4 us (12%)
  other arithmetic  17.9 us (6%)
  between operations  13.8 us (4%)
  local copies, waits for them, and re-layouts  6.9 us (2%)
    unnamed x4, waiting for transfers between devices  139 us
    all_gather x1, waiting for transfers between devices, on_device(): lax.all_gather(half_bf, 'fsdp', axis=0, tiled=True).reshape(-1, LANES)  49.7 us
    all_gather x1, waiting for transfers between devices, on_device(): changes = lax.all_gather(change.astype(BF), 'rep', axis=0, tiled=True)  44.4 us
    pallas_call x1, Pallas kernels, compute(): pl.pallas_call(functools.partial(compute_kernel, seq), grid=(batch,), in_...  38.4 us
    unnamed x11, local copies, waits for them, and re-layouts  6.9 us
  transfers between devices with their start and end apart: 3, of which 3 were waited for; matrix products, arithmetic and copies ran while one was open for 2% of the time, Pallas kernels for 0%

commit v1 on v0

--- a/solution.py
+++ b/solution.py
@@ -226,28 +226,245 @@
     )(images, cotangent, params)
 
 
-def adamw(weight_vals, grad_vals, first_vals, second_vals):
-    first_new = beta_one * first_vals + (1.0 - beta_one) * grad_vals
-    second_new = beta_two * second_vals + (1.0 - beta_two) * grad_vals * grad_vals
-    first_hat = first_new / (1.0 - beta_one**2)
-    second_hat = second_new / (1.0 - beta_two**2)
-    change = -learn_rate * (first_hat / (jnp.sqrt(second_hat) + adam_eps) + decay_rate * weight_vals)
-    return (change, first_new, second_new)
-
-
-def on_device(images, cotangent, weights, first_moment, second_moment):
-    half_bf = weights.astype(BF)
-    params = lax.all_gather(half_bf, "fsdp", axis=0, tiled=True).reshape(-1, LANES)
+MESH = pl.DeviceIdType.MESH
+
+
+def place():
+    f, r = lax.axis_index("fsdp"), lax.axis_index("rep")
+
+    def across(bit):
+        return r + bit * (1 - 2 * ((r // bit) % 2))
+
+    return f, r, across
+
+
+def greet(partners):
+    barrier = pltpu.get_barrier_semaphore()
+    for partner in partners:
+        pl.semaphore_signal(barrier, inc=1, device_id=partner, device_id_type=MESH)
+    pl.semaphore_wait(barrier, len(partners))
+
+
+def gather_kernel(steps, half, out, local_sem, send_sem, recv_sem):
+    f, r, across = place()
+    c, y = r % 2, (r // 2) % 2
+    peer, side, core = (1 - f, r), (f, across(2)), (f, across(1))
+    greet([peer, side, core])
+    mine = (2 * y + c) * steps
+    sides = (2 * (1 - y) + c) * steps
+
+    def copy(src, dst, kind, s, to):
+        return pltpu.make_async_remote_copy(
+            src_ref=src, dst_ref=dst, send_sem=send_sem.at[kind, s], recv_sem=recv_sem.at[kind, s],
+            device_id=to, device_id_type=MESH,
+        )
+
+    first = [copy(half.at[mine + s], out.at[f, mine + s], 0, s, peer) for s in range(steps)]
+    for one in first:
+        one.start()
+    own = pltpu.make_async_copy(half, out.at[f], local_sem)
+    own.start()
+
+    def relay(kind, s, base, to):
+        ref = out.at[1 - f, base + s]
+        return copy(ref, ref, kind, s, to)
+
+    second = [relay(1, s, mine, side) for s in range(steps)]
+    third = [relay(2, s, mine, core) for s in range(steps)]
+    fourth = [relay(3, s, sides, core) for s in range(steps)]
+    for s in range(steps):
+        first[s].wait_recv()
+        second[s].start()
+        third[s].start()
+    for s in range(steps):
+        second[s].wait_recv()
+        fourth[s].start()
+    for s in range(steps):
+        third[s].wait_recv()
+        fourth[s].wait_recv()
+    for group in (first, second, third, fourth):
+        for one in group:
+            one.wait_send()
+    own.wait()
+
+
+def gather_params(half_bf):
+    rows = half_bf.shape[0] // LANES
+    quarter = rows // 4
+    steps = next(s for s in (7, 5, 4, 3, 2, 1) if quarter % (8 * s) == 0)
+    shape = (4 * steps, quarter // steps, LANES)
+    out = pl.pallas_call(
+        functools.partial(gather_kernel, steps),
+        in_specs=[pl.BlockSpec(memory_space=pltpu.VMEM)],
+        out_specs=pl.BlockSpec(memory_space=pltpu.VMEM),
+        out_shape=jax.ShapeDtypeStruct((2,) + shape, BF),
+        scratch_shapes=[
+            pltpu.SemaphoreType.DMA,
+            pltpu.SemaphoreType.DMA((4, steps)),
+            pltpu.SemaphoreType.DMA((4, steps)),
+        ],
+        compiler_params=pltpu.CompilerParams(collective_id=0, has_side_effects=True),
+    )(half_bf.reshape(shape))
+    return out.reshape(2 * rows, LANES)
+
+
+def orders(bits):
+    rest = [b for b in bits if b > 1]
+    low, high = rest[:2], rest[2:]
+    dims = [0] + low
+    return [[1] + dims[i:] + dims[:i] + high for i in range(len(dims))]
+
+
+def reduce_kernel(reps, size, flat, weights, m_in, v_in, new_w, grad, m_out, v_out, acc, sbuf, rbuf, ag, s_send, s_recv, a_send, a_recv):
+    f, r, across = place()
+    bits = [1 << i for i in range(reps.bit_length() - 1)]
+    plans = orders(bits)
+    parts, rows = acc.shape[1], acc.shape[2]
+
+    def bit_of(dim):
+        return f if dim == 0 else (r // dim) % 2
+
+    def stride(dim):
+        return reps if dim == 0 else dim
+
+    def partner(dim):
+        return (1 - f, r) if dim == 0 else (f, across(dim))
+
+    greet([partner(dim) for dim in [0] + bits])
+
+    spans = [(k * rows, min((k + 1) * rows, size)) for k in range(parts)]
+    for p in range(2 * reps):
+        for k, (lo, hi) in enumerate(spans):
+            if hi < lo + rows:
+                acc[p, k] = jnp.zeros((rows, LANES), F32)
+            acc[p, k, 0 : hi - lo, :] = flat[p * size + lo : p * size + hi, :]
+
+    def members(fixed, free):
+        base = sum(value * stride(dim) for dim, value in fixed)
+        out = [base]
+        for dim in free:
+            out = [i + v * stride(dim) for i in out for v in (0, 1)]
+        return out
+
+    pending = {}
+    offsets = [0] * parts
+    depth = len(bits) + 1
+    for stage in range(depth):
+        for k in range(parts):
+            plan = plans[k]
+            dim, free = plan[stage], plan[stage + 1 :]
+            settled = [(d, bit_of(d)) for d in plan[:stage]]
+            if stage:
+                copy, old, count = pending[k]
+                copy.wait_recv()
+                for j, i in enumerate(members(settled, plan[stage:])):
+                    acc[i, k] += rbuf[k, old + j].astype(F32)
+            count = 1 << len(free)
+            start = offsets[k]
+            for j, i in enumerate(members(settled + [(dim, 1 - bit_of(dim))], free)):
+                sbuf[k, start + j] = acc[i, k].astype(BF)
+            copy = pltpu.make_async_remote_copy(
+                src_ref=sbuf.at[k, pl.ds(start, count)], dst_ref=rbuf.at[k, pl.ds(start, count)],
+                send_sem=s_send.at[k, stage], recv_sem=s_recv.at[k, stage],
+                device_id=partner(dim), device_id_type=MESH,
+            )
+            copy.start()
+            pending.setdefault("all", []).append(copy)
+            pending[k] = (copy, start, count)
+            offsets[k] = start + count
+
+    me = f * reps + r
+    waits = []
+    for k in range(parts):
+        copy, old, count = pending[k]
+        copy.wait_recv()
+        lo, hi = spans[k]
+        n = hi - lo
+        g = (acc[me, k] + rbuf[k, old].astype(F32))[:n]
+        grad[lo:hi, :] = g
+        first = beta_one * m_in[lo:hi, :] + (1.0 - beta_one) * g
+        second = beta_two * v_in[lo:hi, :] + (1.0 - beta_two) * g * g
+        m_out[lo:hi, :] = first
+        v_out[lo:hi, :] = second
+        w = weights[pl.ds(r * size + lo, n), :]
+        first_hat = first * (1.0 / (1.0 - beta_one**2))
+        second_hat = second * (1.0 / (1.0 - beta_two**2))
+        change = -learn_rate * (first_hat / (jnp.sqrt(second_hat) + adam_eps) + decay_rate * w)
+        if n < rows:
+            ag[r, k] = jnp.zeros((rows, LANES), BF)
+        ag[r, k, 0:n, :] = change.astype(BF)
+
+    def spread(k, stage):
+        plan = [d for d in plans[k] if d > 0][::-1]
+        dim = plan[stage]
+        fixed = [(d, bit_of(d)) for d in plan[stage:]]
+        copies = []
+        for j, i in enumerate(members(fixed, plan[:stage])):
+            ref = ag.at[i, k]
+            at = (1 << stage) - 1 + j
+            copies.append(
+                pltpu.make_async_remote_copy(
+                    src_ref=ref, dst_ref=ref, send_sem=a_send.at[k, at], recv_sem=a_recv.at[k, at],
+                    device_id=partner(dim), device_id_type=MESH,
+                )
+            )
+        return copies
+
+    last = {k: [] for k in range(parts)}
+    for stage in range(len(bits)):
+        for k in range(parts):
+            for one in last[k]:
+                one.wait_recv()
+            last[k] = spread(k, stage)
+            for one in last[k]:
+                one.start()
+            waits += last[k]
+    for k in range(parts):
+        for one in last[k]:
+            one.wait_recv()
+    for p in range(reps):
+        for k, (lo, hi) in enumerate(spans):
+            at = slice(p * size + lo, p * size + hi)
+            new_w[at, :] = weights[at, :] + ag[p, k][: hi - lo].astype(F32)
+    for one in waits + pending["all"]:
+        one.wait_send()
+
+
+def reduce_update(flat, weights, first_moment, second_moment, reps):
+    size = first_moment.shape[0] // LANES
+    bits = [1 << i for i in range(reps.bit_length() - 1)]
+    parts = len(orders(bits))
+    rows = -(-size // (8 * parts)) * 8
+    piece = jax.ShapeDtypeStruct((size, LANES), F32)
+    stages = len(bits) + 1
+    outs = pl.pallas_call(
+        functools.partial(reduce_kernel, reps, size),
+        in_specs=[pl.BlockSpec(memory_space=pltpu.VMEM)] * 4,
+        out_specs=[pl.BlockSpec(memory_space=pltpu.VMEM)] * 4,
+        out_shape=[jax.ShapeDtypeStruct((reps * size, LANES), F32), piece, piece, piece],
+        scratch_shapes=[
+            pltpu.VMEM((2 * reps, parts, rows, LANES), F32),
+            pltpu.VMEM((parts, 2 * reps - 1, rows, LANES), BF),
+            pltpu.VMEM((parts, 2 * reps - 1, rows, LANES), BF),
+            pltpu.VMEM((reps, parts, rows, LANES), BF),
+            pltpu.SemaphoreType.DMA((parts, stages)),
+            pltpu.SemaphoreType.DMA((parts, stages)),
+            pltpu.SemaphoreType.DMA((parts, reps)),
+            pltpu.SemaphoreType.DMA((parts, reps)),
+        ],
+        compiler_params=pltpu.CompilerParams(
+            collective_id=1, has_side_effects=True, vmem_limit_bytes=60 * 2**20
+        ),
+    )(flat, weights.reshape(-1, LANES), first_moment.reshape(-1, LANES), second_moment.reshape(-1, LANES))
+    return [o.reshape(-1) for o in outs]
+
+
+def on_device(reps, images, cotangent, weights, first_moment, second_moment):
+    params = gather_params(weights.astype(BF))
     output, input_grad, flat_grad = compute(images, cotangent, params)
-    own_grad = lax.psum_scatter(
-        flat_grad.reshape(-1).astype(BF), ("fsdp", "rep"), scatter_dimension=0, tiled=True
-    ).astype(F32)
-    piece_len = first_moment.shape[0]
-    offset = lax.axis_index("rep") * piece_len
-    own_weights = lax.dynamic_slice_in_dim(weights, offset, piece_len)
-    change, new_first, new_second = adamw(own_weights, own_grad, first_moment, second_moment)
-    changes = lax.all_gather(change.astype(BF), "rep", axis=0, tiled=True)
-    new_weights = weights + changes.astype(F32)
+    new_weights, own_grad, new_first, new_second = reduce_update(
+        flat_grad, weights, first_moment, second_moment, reps
+    )
     return (output, input_grad, new_weights, own_grad, new_first, new_second)
 
 
@@ -268,5 +485,5 @@
         P(("fsdp", "rep")),
     )
     return jax.shard_map(
-        on_device, mesh=mesh, in_specs=in_specs, out_specs=out_specs, check_vma=False
+        functools.partial(on_device, mesh.shape["rep"]), mesh=mesh, in_specs=in_specs, out_specs=out_specs, check_vma=False
     )

time: 311 us -> 132 us (0.42)
  waiting for transfers between devices: 233 us -> 0 us
  Pallas kernels: 38.4 us -> 113 us
  other arithmetic: 17.9 us -> 3.39 us
  between operations: 13.8 us -> 0.68 us
  local copies, waits for them, and re-layouts: 6.9 us -> 14.4 us
    unnamed x4 -> x0, waiting for transfers between devices: 139 us -> none
    all_gather x2 -> x0, waiting for transfers between devices: 94.1 us -> none  [the longest x1 49.7 us: on_device(): lax.all_gather(half_bf, 'fsdp', axis=0, tiled=True).reshape(-1, LANES)]
    pallas_call x0 -> x2, Pallas kernels: none -> 74.8 us  [the longest x1 52.5 us: reduce_update(): pl.pallas_call(functools.partial(reduce_kernel, reps, size), in_specs=[pl...]
    convert_element_type x4 -> x1, other arithmetic: 15.8 us -> 3.39 us  [on_device(): params = gather_params(weights.astype(BF))]
    unnamed x11 -> x14, local copies, waits for them, and re-layouts: 6.9 us -> 14.4 us
  transfers between devices with their start and end apart: 3 -> 0, of which waited for: 3 -> 0; matrix products, arithmetic and copies ran while one was open for 2% -> 0% of each run, Pallas kernels for 0% -> 0%
where the time goes in v1:
time: 132 us
  Pallas kernels  113 us (86%)
  local copies, waits for them, and re-layouts  14.4 us (11%)
  other arithmetic  3.39 us (3%)
    pallas_call x1, Pallas kernels, reduce_update(): pl.pallas_call(functools.partial(reduce_kernel, reps, size), in_specs=[pl...  52.5 us
    pallas_call x1, Pallas kernels, compute(): pl.pallas_call(functools.partial(compute_kernel, seq), grid=(batch,), in_...  38.4 us
    pallas_call x1, Pallas kernels, gather_params(): pl.pallas_call(functools.partial(gather_kernel, steps), in_specs=[pl.Bloc...  22.3 us
    unnamed x14, local copies, waits for them, and re-layouts  14.4 us
    convert_element_type x1, other arithmetic, on_device(): params = gather_params(weights.astype(BF))  3.39 us

profile of v1, /device:TPU:1, one launch (start us, length us, event | category | flops | bytes accessed | tf_op | source)
XLA Modules:
  0.0 131.7 jit_solution(14814486995317787470)
XLA Ops:
  0.6 2.0 %copy.11.img = bf16[4,197,384]{2,1,0:T(8,128)(2,1)} copy(bf16[4,197,384]{2,0,1:T(4,128)(2,1)} %param.5) | data formatting | bytes 1210368 | tf_op args[0]
  2.6 2.0 %copy.12.cot = bf16[4,197,384]{2,1,0:T(8,128)(2,1)} copy(bf16[4,197,384]{2,0,1:T(4,128)(2,1)} %param.6) | data formatting | bytes 1210368 | tf_op args[1]
  4.6 3.4 %convert_element_type.3 = bf16[888832]{0:T(1024)(128)(2,1)} convert(f32[888832]{0:T(1024)} %param.7) | non-fusion elementwise | flops 888832 | bytes 5332992 | tf_op jit(solution)/shard_map/convert_element_type | solution.py:463
  8.0 22.3 %shard_map.100 = bf16[2,28,248,128]{3,2,1,0:T(8,128)(2,1)} custom-call(bf16[28,248,128]{2,1,0:T(8,128)(2,1)} %bitcast.11), custom_call_target="tpu_custom_call" | custom-call | tf_op jit(solution)/shard_map/pallas_call | solution.py:296
  30.2 38.4 %shard_map.101 = (bf16[4,197,384]{2,1,0:T(8,128)(2,1)}, bf16[4,197,384]{2,1,0:T(8,128)(2,1)}, f32[13888,128]{1,0:T(8,128)}) custom-call(bf16[4,197,384]{2,1,0:T(8,128)(2,1)} %copy.11.img, bf16[4,197,384]{2,1,0:T(8,128)(2,1)} %copy.12.cot, bf16[13888,128]{1,0:T(8,128)(2,1)} %bitcast.10), custom_call_target="tpu_custom_call" | custom-call | tf_op jit(solution)/shard_map/pallas_call | solution.py:210
  68.7 2.1 %copy.13 = bf16[4,197,384]{2,0,1:T(4,128)(2,1)} copy(bf16[4,197,384]{2,1,0:T(8,128)(2,1)} %get-tuple-element.20) | data formatting | bytes 1210368
  70.8 2.1 %copy.14 = bf16[4,197,384]{2,0,1:T(4,128)(2,1)} copy(bf16[4,197,384]{2,1,0:T(8,128)(2,1)} %get-tuple-element.21) | data formatting | bytes 1210368
  72.9 52.5 %shard_map.102 = (f32[6944,128]{1,0:T(8,128)}, f32[434,128]{1,0:T(8,128)}, f32[434,128]{1,0:T(8,128)}, f32[434,128]{1,0:T(8,128)}) custom-call(f32[13888,128]{1,0:T(8,128)} %get-tuple-element.15.flat, f32[6944,128]{1,0:T(8,128)} %bitcast.9, f32[434,128]{1,0:T(8,128)} %bitcast.16, f32[434,128]{1,0:T(8,128)} %bitcast.17), custom_call_target="tpu_custom_call" | custom-call | tf_op jit(solution)/shard_map/pallas_call | solution.py:440
  125.4 0.0 copy-start.2
  125.4 0.0 copy-start.1
  125.4 0.0 copy-start
  125.4 4.1 %copy.19 = f32[888832]{0:T(1024)} copy(f32[888832]{0:T(1024)} %bitcast.12) | data formatting | bytes 7110656
  129.5 0.0 copy-done.2
  129.5 0.7 copy.20
  130.2 0.0 copy-done.1
  130.2 0.7 copy.21
  130.9 0.0 copy-done
  130.9 0.7 copy.22
Async XLA Ops:
  125.4 4.1 %copy-start.2 = (f32[434,128]{1,0:T(8,128)S(1)}, f32[434,128]{1,0:T(8,128)}, u32[]{:S(2)}) copy-start(f32[434,128]{1,0:T(8,128)} %get-tuple-element.17) | copy-start | bytes 666628
  125.4 4.8 %copy-start.1 = (f32[434,128]{1,0:T(8,128)S(1)}, f32[434,128]{1,0:T(8,128)}, u32[]{:S(2)}) copy-start(f32[434,128]{1,0:T(8,128)} %get-tuple-element.18) | copy-start | bytes 666628
  125.4 5.5 %copy-start = (f32[434,128]{1,0:T(8,128)S(1)}, f32[434,128]{1,0:T(8,128)}, u32[]{:S(2)}) copy-start(f32[434,128]{1,0:T(8,128)} %get-tuple-element.19) | copy-start | bytes 666628

commit v2 on v1

--- a/solution.py
+++ b/solution.py
@@ -222,7 +222,7 @@
         + [pltpu.VMEM(s, F32) for s in mats + vecs]
         + [pltpu.VMEM((pad, width), F32)] * 2
         + [pltpu.VMEM((H, pad, pad), F32)],
-        compiler_params=pltpu.CompilerParams(vmem_limit_bytes=60 * 2**20),
+        compiler_params=pltpu.CompilerParams(vmem_limit_bytes=36 * 2**20),
     )(images, cotangent, params)
 
 
@@ -245,12 +245,21 @@
     pl.semaphore_wait(barrier, len(partners))
 
 
-def gather_kernel(steps, half, out, local_sem, send_sem, recv_sem):
+def gather_kernel(steps, half, out, wide, wide_sem, send_sem, recv_sem):
     f, r, across = place()
     c, y = r % 2, (r // 2) % 2
     peer, side, core = (1 - f, r), (f, across(2)), (f, across(1))
+    mine = (2 * y + c) * steps
+    loads = []
+    for turn in range(4):
+        start = ((2 * y + c + turn) % 4) * steps
+        loads.append(
+            pltpu.make_async_copy(
+                half.at[pl.ds(start, steps)], wide.at[pl.ds(start, steps)], wide_sem.at[turn]
+            )
+        )
+        loads[-1].start()
     greet([peer, side, core])
-    mine = (2 * y + c) * steps
     sides = (2 * (1 - y) + c) * steps
 
     def copy(src, dst, kind, s, to):
@@ -259,11 +268,16 @@
             device_id=to, device_id_type=MESH,
         )
 
-    first = [copy(half.at[mine + s], out.at[f, mine + s], 0, s, peer) for s in range(steps)]
-    for one in first:
-        one.start()
-    own = pltpu.make_async_copy(half, out.at[f], local_sem)
-    own.start()
+    first = [copy(out.at[f, mine + s], out.at[f, mine + s], 0, s, peer) for s in range(steps)]
+    loads[0].wait()
+    for s in range(steps):
+        out[f, mine + s] = wide[mine + s].astype(BF)
+        first[s].start()
+    for turn in range(1, 4):
+        loads[turn].wait()
+        start = ((2 * y + c + turn) % 4) * steps
+        for s in range(steps):
+            out[f, start + s] = wide[start + s].astype(BF)
 
     def relay(kind, s, base, to):
         ref = out.at[1 - f, base + s]
@@ -285,26 +299,26 @@
     for group in (first, second, third, fourth):
         for one in group:
             one.wait_send()
-    own.wait()
-
-
-def gather_params(half_bf):
-    rows = half_bf.shape[0] // LANES
+
+
+def gather_params(half):
+    rows = half.shape[0] // LANES
     quarter = rows // 4
     steps = next(s for s in (7, 5, 4, 3, 2, 1) if quarter % (8 * s) == 0)
     shape = (4 * steps, quarter // steps, LANES)
     out = pl.pallas_call(
         functools.partial(gather_kernel, steps),
-        in_specs=[pl.BlockSpec(memory_space=pltpu.VMEM)],
+        in_specs=[pl.BlockSpec(memory_space=pl.ANY)],
         out_specs=pl.BlockSpec(memory_space=pltpu.VMEM),
         out_shape=jax.ShapeDtypeStruct((2,) + shape, BF),
         scratch_shapes=[
-            pltpu.SemaphoreType.DMA,
+            pltpu.VMEM(shape, F32),
+            pltpu.SemaphoreType.DMA((4,)),
             pltpu.SemaphoreType.DMA((4, steps)),
             pltpu.SemaphoreType.DMA((4, steps)),
         ],
-        compiler_params=pltpu.CompilerParams(collective_id=0, has_side_effects=True),
-    )(half_bf.reshape(shape))
+        compiler_params=pltpu.CompilerParams(collective_id=0, has_side_effects=True, vmem_limit_bytes=16 * 2**20),
+    )(half.reshape(shape))
     return out.reshape(2 * rows, LANES)
 
 
@@ -315,7 +329,9 @@
     return [[1] + dims[i:] + dims[:i] + high for i in range(len(dims))]
 
 
-def reduce_kernel(reps, size, flat, weights, m_in, v_in, new_w, grad, m_out, v_out, acc, sbuf, rbuf, ag, s_send, s_recv, a_send, a_recv):
+def reduce_kernel(
+    reps, size, flat, weights_hbm, m_in, v_in, changes, grad, weights, acc, sbuf, rbuf, ag, w_sem, s_send, s_recv, a_send, a_recv
+):
     f, r, across = place()
     bits = [1 << i for i in range(reps.bit_length() - 1)]
     plans = orders(bits)
@@ -330,6 +346,8 @@
     def partner(dim):
         return (1 - f, r) if dim == 0 else (f, across(dim))
 
+    load = pltpu.make_async_copy(weights_hbm, weights, w_sem)
+    load.start()
     greet([partner(dim) for dim in [0] + bits])
 
     spans = [(k * rows, min((k + 1) * rows, size)) for k in range(parts)]
@@ -375,6 +393,7 @@
 
     me = f * reps + r
     waits = []
+    load.wait()
     for k in range(parts):
         copy, old, count = pending[k]
         copy.wait_recv()
@@ -384,8 +403,6 @@
         grad[lo:hi, :] = g
         first = beta_one * m_in[lo:hi, :] + (1.0 - beta_one) * g
         second = beta_two * v_in[lo:hi, :] + (1.0 - beta_two) * g * g
-        m_out[lo:hi, :] = first
-        v_out[lo:hi, :] = second
         w = weights[pl.ds(r * size + lo, n), :]
         first_hat = first * (1.0 / (1.0 - beta_one**2))
         second_hat = second * (1.0 / (1.0 - beta_two**2))
@@ -425,7 +442,7 @@
     for p in range(reps):
         for k, (lo, hi) in enumerate(spans):
             at = slice(p * size + lo, p * size + hi)
-            new_w[at, :] = weights[at, :] + ag[p, k][: hi - lo].astype(F32)
+            changes[at, :] = ag[p, k][: hi - lo].astype(F32)
     for one in waits + pending["all"]:
         one.wait_send()
 
@@ -437,34 +454,39 @@
     rows = -(-size // (8 * parts)) * 8
     piece = jax.ShapeDtypeStruct((size, LANES), F32)
     stages = len(bits) + 1
+    slots = parts * rows * LANES
+    held = 4 * reps * size * LANES + slots * (2 * reps * 4 + 4 * 2 * (2 * reps - 1) // 2 + 2 * reps) * 17 // 16
     outs = pl.pallas_call(
         functools.partial(reduce_kernel, reps, size),
-        in_specs=[pl.BlockSpec(memory_space=pltpu.VMEM)] * 4,
-        out_specs=[pl.BlockSpec(memory_space=pltpu.VMEM)] * 4,
-        out_shape=[jax.ShapeDtypeStruct((reps * size, LANES), F32), piece, piece, piece],
+        in_specs=[pl.BlockSpec(memory_space=m) for m in (pltpu.VMEM, pl.ANY, pltpu.VMEM, pltpu.VMEM)],
+        out_specs=[pl.BlockSpec(memory_space=pltpu.VMEM)] * 2,
+        out_shape=[jax.ShapeDtypeStruct((reps * size, LANES), F32), piece],
         scratch_shapes=[
+            pltpu.VMEM((reps * size, LANES), F32),
             pltpu.VMEM((2 * reps, parts, rows, LANES), F32),
             pltpu.VMEM((parts, 2 * reps - 1, rows, LANES), BF),
             pltpu.VMEM((parts, 2 * reps - 1, rows, LANES), BF),
             pltpu.VMEM((reps, parts, rows, LANES), BF),
+            pltpu.SemaphoreType.DMA,
             pltpu.SemaphoreType.DMA((parts, stages)),
             pltpu.SemaphoreType.DMA((parts, stages)),
             pltpu.SemaphoreType.DMA((parts, reps)),
             pltpu.SemaphoreType.DMA((parts, reps)),
         ],
         compiler_params=pltpu.CompilerParams(
-            collective_id=1, has_side_effects=True, vmem_limit_bytes=60 * 2**20
+            collective_id=1, has_side_effects=True, vmem_limit_bytes=held + 12 * 2**20
         ),
     )(flat, weights.reshape(-1, LANES), first_moment.reshape(-1, LANES), second_moment.reshape(-1, LANES))
     return [o.reshape(-1) for o in outs]
 
 
 def on_device(reps, images, cotangent, weights, first_moment, second_moment):
-    params = gather_params(weights.astype(BF))
+    params = gather_params(weights)
     output, input_grad, flat_grad = compute(images, cotangent, params)
-    new_weights, own_grad, new_first, new_second = reduce_update(
-        flat_grad, weights, first_moment, second_moment, reps
-    )
+    changes, own_grad = reduce_update(flat_grad, weights, first_moment, second_moment, reps)
+    new_weights = weights + changes
+    new_first = beta_one * first_moment + (1.0 - beta_one) * own_grad
+    new_second = beta_two * second_moment + (1.0 - beta_two) * own_grad * own_grad
     return (output, input_grad, new_weights, own_grad, new_first, new_second)
 
 

time: 132 us -> 111 us (0.84)
  Pallas kernels: 113 us -> 99.9 us
  local copies, waits for them, and re-layouts: 14.4 us -> 7.13 us
    unnamed x14 -> x13, local copies, waits for them, and re-layouts: 14.4 us -> 7.13 us
    pallas_call x1, Pallas kernels: 52.5 us -> 46.9 us  [reduce_update(): pl.pallas_call(functools.partial(reduce_kernel, reps, size), in_specs=[pl...]
    pallas_call x1, Pallas kernels: 38.4 us -> 33.2 us  [compute(): pl.pallas_call(functools.partial(compute_kernel, seq), grid=(batch,), in_...]
    convert_element_type x1 -> x0, other arithmetic: 3.39 us -> none  [on_device(): params = gather_params(weights.astype(BF))]
    add x0 -> x2, other arithmetic: none -> 3.09 us  [the longest x1 2.26 us: on_device(): new_weights = weights + changes]
    pallas_call x1, Pallas kernels: 22.3 us -> 19.8 us  [gather_params(): pl.pallas_call(functools.partial(gather_kernel, steps), in_specs=[pl.Bloc...]
where the time goes in v2:
time: 111 us
  Pallas kernels  99.9 us (90%)
  local copies, waits for them, and re-layouts  7.13 us (6%)
  other arithmetic  3.09 us (3%)
    pallas_call x1, Pallas kernels, reduce_update(): pl.pallas_call(functools.partial(reduce_kernel, reps, size), in_specs=[pl...  46.9 us
    pallas_call x1, Pallas kernels, compute(): pl.pallas_call(functools.partial(compute_kernel, seq), grid=(batch,), in_...  33.2 us
    pallas_call x1, Pallas kernels, gather_params(): pl.pallas_call(functools.partial(gather_kernel, steps), in_specs=[pl.Bloc...  19.8 us
    unnamed x13, local copies, waits for them, and re-layouts  7.13 us
    add x1, other arithmetic, on_device(): new_weights = weights + changes  2.26 us

profile of v2, /device:TPU:1, one launch (start us, length us, event | category | flops | bytes accessed | tf_op | source)
XLA Modules:
  0.0 110.8 jit_solution(17060299493757675605)
XLA Ops:
  0.6 1.1 %copy.11.img = bf16[4,197,384]{2,1,0:T(8,128)(2,1)S(1)} copy(bf16[4,197,384]{2,0,1:T(4,128)(2,1)} %param.5) | data formatting | bytes 1210368 | tf_op args[0]
  1.8 1.1 %copy.12.cot = bf16[4,197,384]{2,1,0:T(8,128)(2,1)S(1)} copy(bf16[4,197,384]{2,0,1:T(4,128)(2,1)} %param.6) | data formatting | bytes 1210368 | tf_op args[1]
  2.9 0.0 copy-start
  2.9 2.0 %copy-done = f32[888832]{0:T(1024)S(1)} copy-done((f32[888832]{0:T(1024)S(1)}, f32[888832]{0:T(1024)}, u32[]{:S(2)}) %copy-start) | copy-done | bytes 3555352
  4.9 19.8 %shard_map.100 = bf16[2,28,248,128]{3,2,1,0:T(8,128)(2,1)S(1)} custom-call(f32[28,248,128]{2,1,0:T(8,128)S(1)} %bitcast.9), custom_call_target="tpu_custom_call" | custom-call | tf_op jit(solution)/shard_map/pallas_call | solution.py:309
  24.7 0.0 copy-start.1
  24.8 0.0 copy-start.2
  24.8 0.0 copy-start.3
  24.8 33.2 %shard_map.101 = (bf16[4,197,384]{2,1,0:T(8,128)(2,1)S(1)}, bf16[4,197,384]{2,1,0:T(8,128)(2,1)S(1)}, f32[13888,128]{1,0:T(8,128)S(1)}) custom-call(bf16[4,197,384]{2,1,0:T(8,128)(2,1)S(1)} %copy.11.img, bf16[4,197,384]{2,1,0:T(8,128)(2,1)S(1)} %copy.12.cot, bf16[13888,128]{1,0:T(8,128)(2,1)S(1)} %bitcast.11), custom_call_target="tpu_custom_call" | custom-call | tf_op jit(solution)/shard_map/pallas_call | solution.py:210
  58.0 1.1 copy.13
  59.0 1.1 copy.14
  60.1 0.0 copy-done.1
  60.1 0.0 copy-done.2
  60.1 0.0 copy-done.3
  60.1 46.9 %shard_map.102 = (f32[6944,128]{1,0:T(8,128)S(1)}, f32[434,128]{1,0:T(8,128)S(1)}) custom-call(f32[13888,128]{1,0:T(8,128)S(1)} %get-tuple-element.13.flat, f32[6944,128]{1,0:T(8,128)S(1)} %bitcast.10, f32[434,128]{1,0:T(8,128)S(1)} %bitcast.13, f32[434,128]{1,0:T(8,128)S(1)} %bitcast.14), custom_call_target="tpu_custom_call" | custom-call | tf_op jit(solution)/shard_map/pallas_call | solution.py:459
  107.0 2.3 %bitcast_add_fusion = f32[888832]{0:T(1024)} fusion(f32[888832]{0:T(1024)S(1)} %copy-done.1, f32[6944,128]{1,0:T(8,128)S(1)} %get-tuple-element.14), kind=kLoop, calls=%fused_computation | loop fusion | flops 888832 | bytes 10665984 | tf_op jit(solution)/shard_map/add | solution.py:487
  109.3 0.8 fusion
  110.1 0.7 copy.16
Async XLA Ops:
  2.9 2.0 %copy-start = (f32[888832]{0:T(1024)S(1)}, f32[888832]{0:T(1024)}, u32[]{:S(2)}) copy-start(f32[888832]{0:T(1024)} %param.7) | copy-start | bytes 10665988
  24.7 35.3 %copy-start.1 = (f32[888832]{0:T(1024)S(1)}, f32[888832]{0:T(1024)}, u32[]{:S(2)}) copy-start(f32[888832]{0:T(1024)} %param.7) | copy-start | bytes 10665988
  24.8 35.3 %copy-start.2 = (f32[55552]{0:T(1024)S(1)}, f32[55552]{0:T(1024)}, u32[]{:S(2)}) copy-start(f32[55552]{0:T(1024)} %param.8) | copy-start | bytes 666628
  24.8 35.3 %copy-start.3 = (f32[55552]{0:T(1024)S(1)}, f32[55552]{0:T(1024)}, u32[]{:S(2)}) copy-start(f32[55552]{0:T(1024)} %param.9) | copy-start | bytes 666628

commit v3 on v2

--- a/solution.py
+++ b/solution.py
@@ -308,7 +308,7 @@
     shape = (4 * steps, quarter // steps, LANES)
     out = pl.pallas_call(
         functools.partial(gather_kernel, steps),
-        in_specs=[pl.BlockSpec(memory_space=pl.ANY)],
+        in_specs=[pl.BlockSpec(memory_space=pltpu.HBM)],
         out_specs=pl.BlockSpec(memory_space=pltpu.VMEM),
         out_shape=jax.ShapeDtypeStruct((2,) + shape, BF),
         scratch_shapes=[
@@ -351,10 +351,12 @@
     greet([partner(dim) for dim in [0] + bits])
 
     spans = [(k * rows, min((k + 1) * rows, size)) for k in range(parts)]
-    for p in range(2 * reps):
-        for k, (lo, hi) in enumerate(spans):
+
+    def pack(k):
+        lo, hi = spans[k]
+        for p in range(2 * reps):
             if hi < lo + rows:
-                acc[p, k] = jnp.zeros((rows, LANES), F32)
+                acc[p, k, (hi - lo) // 8 * 8 :, :] = jnp.zeros((rows - (hi - lo) // 8 * 8, LANES), F32)
             acc[p, k, 0 : hi - lo, :] = flat[p * size + lo : p * size + hi, :]
 
     def members(fixed, free):
@@ -372,7 +374,9 @@
             plan = plans[k]
             dim, free = plan[stage], plan[stage + 1 :]
             settled = [(d, bit_of(d)) for d in plan[:stage]]
-            if stage:
+            if stage == 0:
+                pack(k)
+            else:
                 copy, old, count = pending[k]
                 copy.wait_recv()
                 for j, i in enumerate(members(settled, plan[stage:])):
@@ -392,6 +396,23 @@
             offsets[k] = start + count
 
     me = f * reps + r
+    def spread(k, stage):
+        plan = [d for d in plans[k] if d > 0][::-1]
+        dim = plan[stage]
+        fixed = [(d, bit_of(d)) for d in plan[stage:]]
+        copies = []
+        for j, i in enumerate(members(fixed, plan[:stage])):
+            ref = ag.at[i, k]
+            at = (1 << stage) - 1 + j
+            copies.append(
+                pltpu.make_async_remote_copy(
+                    src_ref=ref, dst_ref=ref, send_sem=a_send.at[k, at], recv_sem=a_recv.at[k, at],
+                    device_id=partner(dim), device_id_type=MESH,
+                )
+            )
+        return copies
+
+    last = {}
     waits = []
     load.wait()
     for k in range(parts):
@@ -410,25 +431,12 @@
         if n < rows:
             ag[r, k] = jnp.zeros((rows, LANES), BF)
         ag[r, k, 0:n, :] = change.astype(BF)
-
-    def spread(k, stage):
-        plan = [d for d in plans[k] if d > 0][::-1]
-        dim = plan[stage]
-        fixed = [(d, bit_of(d)) for d in plan[stage:]]
-        copies = []
-        for j, i in enumerate(members(fixed, plan[:stage])):
-            ref = ag.at[i, k]
-            at = (1 << stage) - 1 + j
-            copies.append(
-                pltpu.make_async_remote_copy(
-                    src_ref=ref, dst_ref=ref, send_sem=a_send.at[k, at], recv_sem=a_recv.at[k, at],
-                    device_id=partner(dim), device_id_type=MESH,
-                )
-            )
-        return copies
-
-    last = {k: [] for k in range(parts)}
-    for stage in range(len(bits)):
+        last[k] = spread(k, 0)
+        for one in last[k]:
+            one.start()
+        waits += last[k]
+
+    for stage in range(1, len(bits)):
         for k in range(parts):
             for one in last[k]:
                 one.wait_recv()
@@ -436,11 +444,10 @@
             for one in last[k]:
                 one.start()
             waits += last[k]
-    for k in range(parts):
+    for k, (lo, hi) in enumerate(spans):
         for one in last[k]:
             one.wait_recv()
-    for p in range(reps):
-        for k, (lo, hi) in enumerate(spans):
+        for p in range(reps):
             at = slice(p * size + lo, p * size + hi)
             changes[at, :] = ag[p, k][: hi - lo].astype(F32)
     for one in waits + pending["all"]:

time: 111 us -> 111 us (level)
  no operation moved by 1% of the time
where the time goes in v3:
time: 111 us; the launch traced here: 110 us
  Pallas kernels  99.4 us (90%)
  local copies, waits for them, and re-layouts  7.13 us (6%)
  other arithmetic  3.09 us (3%)
    pallas_call x1, Pallas kernels, reduce_update(): pl.pallas_call(functools.partial(reduce_kernel, reps, size), in_specs=[pl...  46.4 us
    pallas_call x1, Pallas kernels, compute(): pl.pallas_call(functools.partial(compute_kernel, seq), grid=(batch,), in_...  33.2 us
    pallas_call x1, Pallas kernels, gather_params(): pl.pallas_call(functools.partial(gather_kernel, steps), in_specs=[pl.Bloc...  19.8 us
    unnamed x13, local copies, waits for them, and re-layouts  7.13 us
    add x1, other arithmetic, on_device(): new_weights = weights + changes  2.26 us

profile of v3, /device:TPU:1, one launch (start us, length us, event | category | flops | bytes accessed | tf_op | source)
XLA Modules:
  0.0 110.3 jit_solution(4076330429277674616)
XLA Ops:
  0.6 1.1 %copy.11.img = bf16[4,197,384]{2,1,0:T(8,128)(2,1)S(1)} copy(bf16[4,197,384]{2,0,1:T(4,128)(2,1)} %param.5) | data formatting | bytes 1210368 | tf_op args[0]
  1.8 1.1 %copy.12.cot = bf16[4,197,384]{2,1,0:T(8,128)(2,1)S(1)} copy(bf16[4,197,384]{2,0,1:T(4,128)(2,1)} %param.6) | data formatting | bytes 1210368 | tf_op args[1]
  2.9 0.0 copy-start
  2.9 2.0 %copy-done = f32[888832]{0:T(1024)S(1)} copy-done((f32[888832]{0:T(1024)S(1)}, f32[888832]{0:T(1024)}, u32[]{:S(2)}) %copy-start) | copy-done | bytes 3555352
  4.9 19.8 %shard_map.100 = bf16[2,28,248,128]{3,2,1,0:T(8,128)(2,1)S(1)} custom-call(f32[28,248,128]{2,1,0:T(8,128)S(1)} %bitcast.9), custom_call_target="tpu_custom_call" | custom-call | tf_op jit(solution)/shard_map/pallas_call | solution.py:309
  24.7 0.0 copy-start.1
  24.8 0.0 copy-start.2
  24.8 0.0 copy-start.3
  24.8 33.2 %shard_map.101 = (bf16[4,197,384]{2,1,0:T(8,128)(2,1)S(1)}, bf16[4,197,384]{2,1,0:T(8,128)(2,1)S(1)}, f32[13888,128]{1,0:T(8,128)S(1)}) custom-call(bf16[4,197,384]{2,1,0:T(8,128)(2,1)S(1)} %copy.11.img, bf16[4,197,384]{2,1,0:T(8,128)(2,1)S(1)} %copy.12.cot, bf16[13888,128]{1,0:T(8,128)(2,1)S(1)} %bitcast.11), custom_call_target="tpu_custom_call" | custom-call | tf_op jit(solution)/shard_map/pallas_call | solution.py:210
  58.0 1.1 copy.13
  59.0 1.1 copy.14
  60.1 0.0 copy-done.1
  60.1 0.0 copy-done.2
  60.1 0.0 copy-done.3
  60.1 46.4 %shard_map.102 = (f32[6944,128]{1,0:T(8,128)S(1)}, f32[434,128]{1,0:T(8,128)S(1)}) custom-call(f32[13888,128]{1,0:T(8,128)S(1)} %get-tuple-element.13.flat, f32[6944,128]{1,0:T(8,128)S(1)} %bitcast.10, f32[434,128]{1,0:T(8,128)S(1)} %bitcast.13, f32[434,128]{1,0:T(8,128)S(1)} %bitcast.14), custom_call_target="tpu_custom_call" | custom-call | tf_op jit(solution)/shard_map/pallas_call | solution.py:466
  106.5 2.3 %bitcast_add_fusion = f32[888832]{0:T(1024)} fusion(f32[888832]{0:T(1024)S(1)} %copy-done.1, f32[6944,128]{1,0:T(8,128)S(1)} %get-tuple-element.14), kind=kLoop, calls=%fused_computation | loop fusion | flops 888832 | bytes 10665984 | tf_op jit(solution)/shard_map/add | solution.py:494
  108.8 0.8 fusion
  109.6 0.7 copy.16
Async XLA Ops:
  2.9 2.0 %copy-start = (f32[888832]{0:T(1024)S(1)}, f32[888832]{0:T(1024)}, u32[]{:S(2)}) copy-start(f32[888832]{0:T(1024)} %param.7) | copy-start | bytes 10665988
  24.7 35.3 %copy-start.1 = (f32[888832]{0:T(1024)S(1)}, f32[888832]{0:T(1024)}, u32[]{:S(2)}) copy-start(f32[888832]{0:T(1024)} %param.7) | copy-start | bytes 10665988
  24.8 35.3 %copy-start.2 = (f32[55552]{0:T(1024)S(1)}, f32[55552]{0:T(1024)}, u32[]{:S(2)}) copy-start(f32[55552]{0:T(1024)} %param.8) | copy-start | bytes 666628
  24.8 35.3 %copy-start.3 = (f32[55552]{0:T(1024)S(1)}, f32[55552]{0:T(1024)}, u32[]{:S(2)}) copy-start(f32[55552]{0:T(1024)} %param.9) | copy-start | bytes 666628

commit v4 on v3

--- a/solution.py
+++ b/solution.py
@@ -123,7 +123,7 @@
     dout = dout_f.astype(BF)
     result = resid + vec[7:8, :]
     dnorm2 = None
-    step = 512
+    step = 768
     for c in range(0, FF, step):
         cut = slice(c, c + step)
         pre = nn(normed2, w1[:, cut]) + b1[:, cut]

time: 111 us -> 109 us (0.982)
  Pallas kernels: 99.4 us -> 97.6 us
    pallas_call x1, Pallas kernels: 33.2 us -> 31.5 us  [compute(): pl.pallas_call(functools.partial(compute_kernel, seq), grid=(batch,), in_...]
where the time goes in v4:
time: 109 us
  Pallas kernels  97.6 us (90%)
  local copies, waits for them, and re-layouts  7.13 us (7%)
  other arithmetic  3.09 us (3%)
    pallas_call x1, Pallas kernels, reduce_update(): pl.pallas_call(functools.partial(reduce_kernel, reps, size), in_specs=[pl...  46.3 us
    pallas_call x1, Pallas kernels, compute(): pl.pallas_call(functools.partial(compute_kernel, seq), grid=(batch,), in_...  31.5 us
    pallas_call x1, Pallas kernels, gather_params(): pl.pallas_call(functools.partial(gather_kernel, steps), in_specs=[pl.Bloc...  19.8 us
    unnamed x13, local copies, waits for them, and re-layouts  7.13 us
    add x1, other arithmetic, on_device(): new_weights = weights + changes  2.26 us

profile of v4, /device:TPU:1, one launch (start us, length us, event | category | flops | bytes accessed | tf_op | source)
XLA Modules:
  0.0 108.5 jit_solution(10026316425499833946)
XLA Ops:
  0.6 1.1 %copy.11.img = bf16[4,197,384]{2,1,0:T(8,128)(2,1)S(1)} copy(bf16[4,197,384]{2,0,1:T(4,128)(2,1)} %param.5) | data formatting | bytes 1210368 | tf_op args[0]
  1.8 1.1 %copy.12.cot = bf16[4,197,384]{2,1,0:T(8,128)(2,1)S(1)} copy(bf16[4,197,384]{2,0,1:T(4,128)(2,1)} %param.6) | data formatting | bytes 1210368 | tf_op args[1]
  2.9 0.0 copy-start
  2.9 2.0 %copy-done = f32[888832]{0:T(1024)S(1)} copy-done((f32[888832]{0:T(1024)S(1)}, f32[888832]{0:T(1024)}, u32[]{:S(2)}) %copy-start) | copy-done | bytes 3555352
  4.9 19.8 %shard_map.100 = bf16[2,28,248,128]{3,2,1,0:T(8,128)(2,1)S(1)} custom-call(f32[28,248,128]{2,1,0:T(8,128)S(1)} %bitcast.9), custom_call_target="tpu_custom_call" | custom-call | tf_op jit(solution)/shard_map/pallas_call | solution.py:309
  24.7 0.0 copy-start.1
  24.8 0.0 copy-start.2
  24.8 0.0 copy-start.3
  24.8 31.5 %shard_map.101 = (bf16[4,197,384]{2,1,0:T(8,128)(2,1)S(1)}, bf16[4,197,384]{2,1,0:T(8,128)(2,1)S(1)}, f32[13888,128]{1,0:T(8,128)S(1)}) custom-call(bf16[4,197,384]{2,1,0:T(8,128)(2,1)S(1)} %copy.11.img, bf16[4,197,384]{2,1,0:T(8,128)(2,1)S(1)} %copy.12.cot, bf16[13888,128]{1,0:T(8,128)(2,1)S(1)} %bitcast.11), custom_call_target="tpu_custom_call" | custom-call | tf_op jit(solution)/shard_map/pallas_call | solution.py:210
  56.2 1.1 copy.13
  57.3 1.1 copy.14
  58.3 0.0 copy-done.1
  58.4 0.0 copy-done.2
  58.4 0.0 copy-done.3
  58.4 46.3 %shard_map.102 = (f32[6944,128]{1,0:T(8,128)S(1)}, f32[434,128]{1,0:T(8,128)S(1)}) custom-call(f32[13888,128]{1,0:T(8,128)S(1)} %get-tuple-element.13.flat, f32[6944,128]{1,0:T(8,128)S(1)} %bitcast.10, f32[434,128]{1,0:T(8,128)S(1)} %bitcast.13, f32[434,128]{1,0:T(8,128)S(1)} %bitcast.14), custom_call_target="tpu_custom_call" | custom-call | tf_op jit(solution)/shard_map/pallas_call | solution.py:466
  104.7 2.3 %bitcast_add_fusion = f32[888832]{0:T(1024)} fusion(f32[888832]{0:T(1024)S(1)} %copy-done.1, f32[6944,128]{1,0:T(8,128)S(1)} %get-tuple-element.14), kind=kLoop, calls=%fused_computation | loop fusion | flops 888832 | bytes 10665984 | tf_op jit(solution)/shard_map/add | solution.py:494
  107.0 0.8 fusion
  107.8 0.7 copy.16
Async XLA Ops:
  2.9 2.0 %copy-start = (f32[888832]{0:T(1024)S(1)}, f32[888832]{0:T(1024)}, u32[]{:S(2)}) copy-start(f32[888832]{0:T(1024)} %param.7) | copy-start | bytes 10665988
  24.7 33.6 %copy-start.1 = (f32[888832]{0:T(1024)S(1)}, f32[888832]{0:T(1024)}, u32[]{:S(2)}) copy-start(f32[888832]{0:T(1024)} %param.7) | copy-start | bytes 10665988
  24.8 33.6 %copy-start.2 = (f32[55552]{0:T(1024)S(1)}, f32[55552]{0:T(1024)}, u32[]{:S(2)}) copy-start(f32[55552]{0:T(1024)} %param.8) | copy-start | bytes 666628
  24.8 33.6 %copy-start.3 = (f32[55552]{0:T(1024)S(1)}, f32[55552]{0:T(1024)}, u32[]{:S(2)}) copy-start(f32[55552]{0:T(1024)} %param.9) | copy-start | bytes 666628
